TPU v7x, 32 devices: a whole 2x2x4 slice. The times are simulated.
32 devices in a mesh: wide: 8 (over y, x, core), narrow: 4 (over z).
Axes of the slice: x: 2, y: 2, z: 4, core: 2. Of those that a mesh axis runs over, the one named last changes fastest.
Arguments:
- events: bfloat16 [8192, 1024], P('wide'), may hold values from -36 to 36
- lengths: int32 [24], replicated, may hold values from 1 to 2048, 8192 in all
- in_gain: float32 [1024], replicated, may hold values from 0.1 to 1.9
- w_uvqk: bfloat16 [1024, 8, 512], P(None, 'narrow'), may hold values from -2 to 2, as said below
- out_gain: float32 [8, 128], P('narrow'), may hold values from 0.1 to 1.9
- w_out: bfloat16 [8, 128, 1024], P('narrow'), may hold values from -0.25 to 0.25
Outputs:
- layer_out: bfloat16 [8192, 1024], P('wide', 'narrow')
Inputs may be any that keep to these rules, and one draw needn't show every extreme that they name: `w_uvqk`: projection weights.
All inputs are finite; a program needn't handle non-finite values.
Results may differ from a plain program's by a relative error of at most 0.0036.
Values may be sent and summed in bfloat16 or wider, within the bound.
A program may use at most 64 MiB of HBM per device.

v0:
```python
import jax
import jax.numpy as jnp
from jax import lax
from jax.sharding import PartitionSpec as P


def from_behind(value, axis, steps):
    count = lax.axis_size(axis)
    initial, last = (max(0, -steps), min(count, count - steps))
    return lax.ppermute(value, axis, [(source, source + steps) for source in range(initial, last)])


def fetch_relay(pair):
    return from_behind((pair[0], pair[1]), "wide", 1)


def on_device(events, lengths, in_gain, w_uvqk, out_gain, w_out):
    rows_w = events.shape[0]
    heads_local = w_uvqk.shape[1]
    head_size = out_gain.shape[1]
    events_f = events.astype(jnp.float32)
    average = jnp.mean(events_f, axis=-1, keepdims=True)
    variance = jnp.mean((events_f - average) ** 2, axis=-1, keepdims=True)
    normed = ((events_f - average) * lax.rsqrt(variance + 1e-05) * in_gain).astype(jnp.bfloat16)
    projected = jnp.einsum("rd,dhc->rhc", normed, w_uvqk, preferred_element_type=jnp.float32)
    projected = jax.nn.silu(projected).astype(jnp.bfloat16)
    update_gate = projected[:, :, :head_size]
    values_own = projected[:, :, head_size : 2 * head_size]
    queries = projected[:, :, 2 * head_size : 3 * head_size]
    keys_own = projected[:, :, 3 * head_size :]
    user_ends = jnp.cumsum(lengths)

    def owner_of(grow):
        return jnp.sum((user_ends[None, :] <= grow[:, None]).astype(jnp.int32), axis=1)

    first_row = lax.axis_index("wide") * rows_w
    query_pos = first_row + jnp.arange(rows_w, dtype=jnp.int32)
    query_user = owner_of(query_pos)
    scaling = head_size ** (-0.5)

    def attend(running, key_rows, value_rows, key_first):
        key_count = key_rows.shape[0]
        block_rows = 512

        def block_step(carry, block_index):
            key_start = block_index * block_rows
            key_block = lax.dynamic_slice_in_dim(key_rows, key_start, block_rows, 0)
            value_block = lax.dynamic_slice_in_dim(value_rows, key_start, block_rows, 0)
            key_pos = key_first + key_start + jnp.arange(block_rows, dtype=jnp.int32)
            key_user = owner_of(key_pos)
            allowed = (
                (key_user[None, :] == query_user[:, None])
                & (key_pos[None, :] <= query_pos[:, None])
                & (key_pos[None, :] >= 0)
            )
            scores = (
                jnp.einsum("rhc,khc->hrk", queries, key_block, preferred_element_type=jnp.float32)
                * scaling
            )
            weights = jnp.where(allowed[None], jax.nn.silu(scores), 0.0).astype(jnp.bfloat16)
            carry = carry + jnp.einsum(
                "hrk,khc->rhc", weights, value_block, preferred_element_type=jnp.float32
            )
            return (carry, None)

        running, _ = lax.scan(
            block_step, running, jnp.arange(key_count // block_rows, dtype=jnp.int32)
        )
        return running

    attended = attend(
        jnp.zeros((rows_w, heads_local, head_size), jnp.float32), keys_own, values_own, first_row
    )
    reach = lax.axis_size("wide") // 4

    def relay_turn(turn_index, carry):
        keys_held, values_held, running = carry
        keys_held, values_held = fetch_relay((keys_held, values_held))
        running = attend(running, keys_held, values_held, first_row - turn_index * rows_w)
        return (keys_held, values_held, running)

    _, _, attended = lax.fori_loop(1, reach + 1, relay_turn, (keys_own, values_own, attended))
    centre = jnp.mean(attended, axis=-1, keepdims=True)
    deviation = jnp.mean((attended - centre) ** 2, axis=-1, keepdims=True)
    gated = (
        (attended - centre)
        * lax.rsqrt(deviation + 1e-05)
        * out_gain[None]
        * update_gate.astype(jnp.float32)
    )
    gated = gated.astype(jnp.bfloat16)
    columns = lax.all_to_all(w_out, "narrow", split_axis=2, concat_axis=0, tiled=True)
    summed = jnp.einsum(
        "rhc,hcd->rd",
        lax.all_gather(gated, "narrow", axis=1, tiled=True),
        columns,
        preferred_element_type=jnp.float32,
    )
    share = summed.shape[1]
    own_cols = lax.dynamic_slice_in_dim(events_f, lax.axis_index("narrow") * share, share, 1)
    return (own_cols + summed).astype(jnp.bfloat16)


def solution(mesh):
    in_specs = (
        P("wide", None),
        P(),
        P(),
        P(None, "narrow", None),
        P("narrow", None),
        P("narrow", None, None),
    )
    out_specs = P("wide", "narrow")
    return jax.shard_map(
        on_device, mesh=mesh, in_specs=in_specs, out_specs=out_specs, check_vma=False
    )
```

profile of v0, /device:TPU:3, one launch (start us, length us, event | category | flops | bytes accessed | tf_op | source)
XLA Modules:
  0.0 165.2 jit_solution(15008756031488288233)
XLA Ops:
  6.6 2.1 %convert_reduce_fusion.2 = f32[1024]{0:T(1024)S(1)} fusion(bf16[1024,1024]{1,0:T(8,128)(2,1)} %param.12), kind=kLoop, calls=%fused_computation.47 | loop fusion | flops 2096128 | bytes 2101248 | tf_op jit(solution)/shard_map/reduce_sum | solution.py:22
  8.6 2.3 %multiply_reduce_fusion = f32[1024]{0:T(1024)S(1)} fusion(bf16[1024,1024]{1,0:T(8,128)(2,1)} %param.12, f32[1024]{0:T(1024)S(1)} %broadcast_multiply_fusion.1), kind=kLoop, calls=%fused_computation.46 | loop fusion | flops 4193280 | bytes 2105344 | tf_op jit(solution)/shard_map/reduce_sum | solution.py:23
  11.0 3.4 %multiply_convert_fusion = bf16[1024,2,512]{2,0,1:T(8,128)(2,1)S(1)} fusion(bf16[1024,2,512]{2,1,0:T(2,128)(2,1)S(1)} %copy-done, bf16[1024,1024]{1,0:T(8,128)(2,1)S(1)} %copy-done.1, f32[1024]{0:T(1024)S(1)} %copy-done.5, f32[1024]{0:T(1024)S(1)} %add_rsqrt_fusion.1, f32[1024]{0:T(1024)S(1)} %broadcast_multiply_fusion.1), kind=kOutput, calls=%fused_computation.44 | convolution fusion | flops 2157969408 | bytes 6303744 | tf_op jit(solution)/shard_map/rd,dhc->rhc/dot_general | solution.py:25
  14.4 1.3 copy-done.2
  15.7 1.2 fusion.49
  17.6 12.9 %while.56 = (s32[]{:T(128)}, f32[1024,2,128]{0,2,1:T(8,128)}, s32[2]{0:T(128)S(1)}, bf16[1024,2,128]{0,2,1:T(8,128)(2,1)S(1)}, s32[24]{0:T(128)S(1)}, /*index=5*...) while((s32[]{:T(128)}, f32[1024,2,128]{0,2,1:T(8,128)}, ...), condition=%wide.region_6.7_spmd.clone.clone.clone, body=%wide.region_4.6_spmd.clone.clone.clone.sunk | while | flops 546871296 | bytes 4219704 | solution.py:66
  17.6 0.7 dynamic_slice.51
  19.1 0.6 and_and_fusion.4
  19.6 4.2 %fusion.65 = f32[1024,2,128]{0,2,1:T(8,128)} fusion(bf16[1024,2,128]{2,0,1:T(8,128)(2,1)} %get-tuple-element.781, pred[1024,512]{0,1:T(8,128)(4,1)S(1)} %and_and_fusion.4, f32[1024,2,128]{0,2,1:T(8,128)} %get-tuple-element.761, pred[]{:T(512)S(6)} %compare.5, bf16[1024,2,128]{2,0,1:T(8,128)(2,1)} %get-tuple-element.780, s32[]{:T(128)S(6)} %select_n.48, ...), kind=kOutput, calls=%fused_computation.33.clone.1 | convolution fusion | flops 544735232 | bytes 3671552 | tf_op jit(solution)/shard_map/while/body/eval_jaxpr/hrk,khc->rhc/dot_general | solution.py:61
  23.9 0.7 dynamic_slice.51
  25.9 4.6 %fusion.65 = f32[1024,2,128]{0,2,1:T(8,128)} fusion(bf16[1024,2,128]{2,0,1:T(8,128)(2,1)} %get-tuple-element.781, pred[1024,512]{0,1:T(8,128)(4,1)S(1)} %and_and_fusion.4, f32[1024,2,128]{0,2,1:T(8,128)} %get-tuple-element.761, pred[]{:T(512)S(6)} %compare.5, bf16[1024,2,128]{2,0,1:T(8,128)(2,1)} %get-tuple-element.780, s32[]{:T(128)S(6)} %select_n.48, ...), kind=kOutput, calls=%fused_computation.33.clone.1 | convolution fusion | flops 544735232 | bytes 3671552 | tf_op jit(solution)/shard_map/while/body/eval_jaxpr/hrk,khc->rhc/dot_general | solution.py:61
  30.5 62.6 %while.55 = (s32[]{:T(128)}, bf16[1024,2,128]{2,0,1:T(8,128)(2,1)}, bf16[1024,2,128]{0,2,1:T(8,128)(2,1)S(1)}, f32[1024,2,128]{0,2,1:T(8,128)}, s32[]{:T(128)}, ...) while((s32[]{:T(128)}, bf16[1024,2,128]{2,0,1:T(8,128)(2,1)}, ...), condition=%wide.region_11.12_spmd.clone.clone, body=%wide.region_7.11_spmd.clone.clone.sunk | while | flops 546609152 | bytes 10511020 | solution.py:82
  30.5 3.7 %collective-permute-start = (bf16[1024,2,128]{2,0,1:T(8,128)(2,1)}, bf16[1024,2,128]{2,0,1:T(8,128)(2,1)S(1)}, u32[]{:S(2)}, u32[]{:S(2)}) collective-permute-start(bf16[1024,2,128]{2,0,1:T(8,128)(2,1)} %get-tuple-element.802), channel_id=1, source_target_pairs={{0,4},{4,8},{8,12},{12,16},{16,20},{20,24},{24,28},{1,5},{5,9},{9,... | collective-permute-start | bytes 1572872 | tf_op jit(solution)/shard_map/while/body/eval_jaxpr/ppermute | solution.py:10
  34.2 1.9 %collective-permute-start.1 = (bf16[1024,2,128]{0,2,1:T(8,128)(2,1)S(1)}, bf16[1024,2,128]{0,2,1:T(8,128)(2,1)}, u32[]{:S(2)}, u32[]{:S(2)}) collective-permute-start(bf16[1024,2,128]{0,2,1:T(8,128)(2,1)S(1)} %get-tuple-element.803), channel_id=1, source_target_pairs={{0,4},{4,8},{8,12},{12,16},{16,20},{20,24},{24,28},{1,5},{5,9},{9,... | collective-permute-start | bytes 1572872 | tf_op jit(solution)/shard_map/while/body/eval_jaxpr/ppermute | solution.py:10
  36.1 4.5 %collective-permute-done = bf16[1024,2,128]{2,0,1:T(8,128)(2,1)S(1)} collective-permute-done((bf16[1024,2,128]{2,0,1:T(8,128)(2,1)}, bf16[1024,2,128]{2,0,1:T(8,128)(2,1)S(1)}, u32[]{:S(2)}, u32[]{:S(2)}) %collective-permute-start) | collective-permute-done | bytes 524320 | tf_op jit(solution)/shard_map/while/body/eval_jaxpr/ppermute | solution.py:10
  40.6 5.5 %collective-permute-done.1 = bf16[1024,2,128]{0,2,1:T(8,128)(2,1)} collective-permute-done((bf16[1024,2,128]{0,2,1:T(8,128)(2,1)S(1)}, bf16[1024,2,128]{0,2,1:T(8,128)(2,1)}, u32[]{:S(2)}, u32[]{:S(2)}) %collective-permute-start.1) | collective-permute-done | bytes 524320 | tf_op jit(solution)/shard_map/while/body/eval_jaxpr/ppermute | solution.py:10
  46.1 13.0 %while.57 = (s32[]{:T(128)}, f32[1024,2,128]{0,2,1:T(8,128)}, s32[2]{0:T(128)S(1)}, bf16[1024,2,128]{0,2,1:T(8,128)(2,1)}, s32[24]{0:T(128)S(1)}, /*index=5*/s32...) while((s32[]{:T(128)}, f32[1024,2,128]{0,2,1:T(8,128)}, ...), condition=%wide.region_10.10_spmd, body=%wide.region_8.9_spmd.sunk | while | flops 546608128 | bytes 4215091 | solution.py:66
  46.1 0.6 dynamic_slice.54
  47.4 0.6 and_and_fusion.5
  48.0 4.6 %fusion.69 = f32[1024,2,128]{0,2,1:T(8,128)} fusion(f32[1024,2,128]{0,2,1:T(8,128)} %get-tuple-element.720, bf16[1024,2,128]{2,0,1:T(8,128)(2,1)} %get-tuple-element.742, pred[1024,512]{0,1:T(8,128)(4,1)S(1)} %and_and_fusion.5, bf16[1024,2,128]{2,0,1:T(8,128)(2,1)S(1)} %get-tuple-element.741, s32[]{:T(128)S(6)} %select_n.50, ...), kind=kOutput, calls=%fused_computation.12.clone.1 | convolution fusion | flops 544473088 | bytes 3671040 | tf_op jit(solution)/shard_map/while/body/eval_jaxpr/while/body/eval_jaxpr/hrk,khc->rhc/dot_general | solution.py:61
  52.6 0.6 dynamic_slice.54
  54.0 0.6 and_and_fusion.5
  54.5 4.6 %fusion.69 = f32[1024,2,128]{0,2,1:T(8,128)} fusion(f32[1024,2,128]{0,2,1:T(8,128)} %get-tuple-element.720, bf16[1024,2,128]{2,0,1:T(8,128)(2,1)} %get-tuple-element.742, pred[1024,512]{0,1:T(8,128)(4,1)S(1)} %and_and_fusion.5, bf16[1024,2,128]{2,0,1:T(8,128)(2,1)S(1)} %get-tuple-element.741, s32[]{:T(128)S(6)} %select_n.50, ...), kind=kOutput, calls=%fused_computation.12.clone.1 | convolution fusion | flops 544473088 | bytes 3671040 | tf_op jit(solution)/shard_map/while/body/eval_jaxpr/while/body/eval_jaxpr/hrk,khc->rhc/dot_general | solution.py:61
  59.1 0.8 copy.68
  59.9 1.0 copy.69
  60.9 5.4 %collective-permute-start = (bf16[1024,2,128]{2,0,1:T(8,128)(2,1)}, bf16[1024,2,128]{2,0,1:T(8,128)(2,1)S(1)}, u32[]{:S(2)}, u32[]{:S(2)}) collective-permute-start(bf16[1024,2,128]{2,0,1:T(8,128)(2,1)} %get-tuple-element.802), channel_id=1, source_target_pairs={{0,4},{4,8},{8,12},{12,16},{16,20},{20,24},{24,28},{1,5},{5,9},{9,... | collective-permute-start | bytes 1572872 | tf_op jit(solution)/shard_map/while/body/eval_jaxpr/ppermute | solution.py:10
  66.3 1.9 %collective-permute-start.1 = (bf16[1024,2,128]{0,2,1:T(8,128)(2,1)S(1)}, bf16[1024,2,128]{0,2,1:T(8,128)(2,1)}, u32[]{:S(2)}, u32[]{:S(2)}) collective-permute-start(bf16[1024,2,128]{0,2,1:T(8,128)(2,1)S(1)} %get-tuple-element.803), channel_id=1, source_target_pairs={{0,4},{4,8},{8,12},{12,16},{16,20},{20,24},{24,28},{1,5},{5,9},{9,... | collective-permute-start | bytes 1572872 | tf_op jit(solution)/shard_map/while/body/eval_jaxpr/ppermute | solution.py:10
  68.3 4.5 %collective-permute-done = bf16[1024,2,128]{2,0,1:T(8,128)(2,1)S(1)} collective-permute-done((bf16[1024,2,128]{2,0,1:T(8,128)(2,1)}, bf16[1024,2,128]{2,0,1:T(8,128)(2,1)S(1)}, u32[]{:S(2)}, u32[]{:S(2)}) %collective-permute-start) | collective-permute-done | bytes 524320 | tf_op jit(solution)/shard_map/while/body/eval_jaxpr/ppermute | solution.py:10
  72.7 5.5 %collective-permute-done.1 = bf16[1024,2,128]{0,2,1:T(8,128)(2,1)} collective-permute-done((bf16[1024,2,128]{0,2,1:T(8,128)(2,1)S(1)}, bf16[1024,2,128]{0,2,1:T(8,128)(2,1)}, u32[]{:S(2)}, u32[]{:S(2)}) %collective-permute-start.1) | collective-permute-done | bytes 524320 | tf_op jit(solution)/shard_map/while/body/eval_jaxpr/ppermute | solution.py:10
  78.3 13.0 %while.57 = (s32[]{:T(128)}, f32[1024,2,128]{0,2,1:T(8,128)}, s32[2]{0:T(128)S(1)}, bf16[1024,2,128]{0,2,1:T(8,128)(2,1)}, s32[24]{0:T(128)S(1)}, /*index=5*/s32...) while((s32[]{:T(128)}, f32[1024,2,128]{0,2,1:T(8,128)}, ...), condition=%wide.region_10.10_spmd, body=%wide.region_8.9_spmd.sunk | while | flops 546608128 | bytes 4215091 | solution.py:66
  78.3 0.6 dynamic_slice.54
  79.6 0.6 and_and_fusion.5
  80.2 4.6 %fusion.69 = f32[1024,2,128]{0,2,1:T(8,128)} fusion(f32[1024,2,128]{0,2,1:T(8,128)} %get-tuple-element.720, bf16[1024,2,128]{2,0,1:T(8,128)(2,1)} %get-tuple-element.742, pred[1024,512]{0,1:T(8,128)(4,1)S(1)} %and_and_fusion.5, bf16[1024,2,128]{2,0,1:T(8,128)(2,1)S(1)} %get-tuple-element.741, s32[]{:T(128)S(6)} %select_n.50, ...), kind=kOutput, calls=%fused_computation.12.clone.1 | convolution fusion | flops 544473088 | bytes 3671040 | tf_op jit(solution)/shard_map/while/body/eval_jaxpr/while/body/eval_jaxpr/hrk,khc->rhc/dot_general | solution.py:61
  84.8 0.6 dynamic_slice.54
  86.1 0.6 and_and_fusion.5
  86.7 4.6 %fusion.69 = f32[1024,2,128]{0,2,1:T(8,128)} fusion(f32[1024,2,128]{0,2,1:T(8,128)} %get-tuple-element.720, bf16[1024,2,128]{2,0,1:T(8,128)(2,1)} %get-tuple-element.742, pred[1024,512]{0,1:T(8,128)(4,1)S(1)} %and_and_fusion.5, bf16[1024,2,128]{2,0,1:T(8,128)(2,1)S(1)} %get-tuple-element.741, s32[]{:T(128)S(6)} %select_n.50, ...), kind=kOutput, calls=%fused_computation.12.clone.1 | convolution fusion | flops 544473088 | bytes 3671040 | tf_op jit(solution)/shard_map/while/body/eval_jaxpr/while/body/eval_jaxpr/hrk,khc->rhc/dot_general | solution.py:61
  91.3 0.8 copy.68
  92.1 1.0 copy.69
  93.1 1.6 copy.38
  94.7 1.3 reduce_sum.66
  96.0 0.6 multiply_reduce_fusion.1
  96.7 2.4 %multiply_convert_fusion.2 = bf16[1024,2,128]{2,0,1:T(8,128)(2,1)} fusion(f32[1024,2,128]{2,0,1:T(8,128)S(1)} %copy.38, bf16[1024,2,512]{2,0,1:T(8,128)(2,1)} %copy-done.2, f32[2,128]{1,0:T(2,128)S(1)} %copy-done.3, f32[1024,2]{0,1:T(2,128)S(1)} %add_rsqrt_fusion, f32[1024,2]{0,1:T(2,128)S(1)} %broadcast_multiply_fusion), kind=kLoop, calls=%fused_computation.57 | loop fusion | flops 1572864 | bytes 2114560 | tf_op jit(solution)/shard_map/convert_element_type | solution.py:91
  99.0 2.0 %copy.39 = bf16[2,128,1024]{1,0,2:T(2,128)(2,1)} copy(bf16[2,128,1024]{2,1,0:T(8,128)(2,1)} %param.17) | data formatting | bytes 1048576 | tf_op args[5]
  101.1 4.6 %all-to-all-start = ((bf16[2,128,1024]{1,0,2:T(2,128)(2,1)}), bf16[2,128,1024]{1,0,2:T(2,128)(2,1)S(1)}, u32[]{:S(2)}, u32[]{:S(2)}) async-start(bf16[2,128,1024]{1,0,2:T(2,128)(2,1)} %copy.39), calls=%async_computation | async-start | bytes 1048576 | tf_op jit(solution)/shard_map/all_to_all | solution.py:92
  105.7 4.0 %convert_element_type.33 = f32[1024,1024]{1,0:T(8,128)} convert(bf16[1024,1024]{1,0:T(8,128)(2,1)} %param.12) | non-fusion elementwise | flops 1048576 | bytes 6291456 | tf_op jit(solution)/shard_map/convert_element_type | solution.py:21
  109.6 17.5 %all-to-all-done = bf16[2,128,1024]{1,0,2:T(2,128)(2,1)S(1)} async-done(((bf16[2,128,1024]{1,0,2:T(2,128)(2,1)}), bf16[2,128,1024]{1,0,2:T(2,128)(2,1)S(1)}, u32[]{:S(2)}, u32[]{:S(2)}) %all-to-all-start) | async-done | bytes 524320 | tf_op jit(solution)/shard_map/all_to_all | solution.py:92
  127.5 27.4 %all-gather.2.cloned.1.call-done = bf16[1024,8,128]{2,0,1:T(8,128)(2,1)} async-done(((bf16[1024,2,128]{2,0,1:T(8,128)(2,1)}), bf16[1024,8,128]{2,0,1:T(8,128)(2,1)}) %all-gather.2.cloned.1.call-update) | async-done | bytes 2097168 | tf_op jit(solution)/shard_map/all_gather | solution.py:95
  154.9 3.4 %fusion.48 = bf16[1024,256]{1,0:T(8,128)(2,1)} fusion(bf16[1024,8,128]{2,0,1:T(8,128)(2,1)} %all-gather.2.cloned.1.call-done, bf16[8,128,256]{2,1,0:T(8,128)(2,1)S(1)} %bitcast.89, f32[1024,1024]{1,0:T(8,128)} %convert_element_type.33, s32[]{:T(128)S(6)} %select_n.18), kind=kOutput, calls=%fused_computation.56 | convolution fusion | flops 537395200 | bytes 4194308 | tf_op jit(solution)/shard_map/rhc,hcd->rd/dot_general | solution.py:93
  (51 shorter events, 2.2 us)
Async XLA Ops:
  6.5 4.4 %copy-start = (bf16[1024,2,512]{2,1,0:T(2,128)(2,1)S(1)}, bf16[1024,2,512]{2,1,0:T(2,128)(2,1)}, u32[]{:S(2)}) copy-start(bf16[1024,2,512]{2,1,0:T(2,128)(2,1)} %param.15) | copy-start | bytes 6291460
  6.5 4.4 %copy-start.5 = (f32[1024]{0:T(1024)S(1)}, f32[1024]{0:T(1024)}, u32[]{:S(2)}) copy-start(f32[1024]{0:T(1024)} %param.14) | copy-start | bytes 12292
  6.5 148.4 %all-gather.2.cloned.1.call-start = ((), (), s32[]{:S(2)}) async-start(), calls=%async_computation.1 | async-start | bytes 2621440 | tf_op jit(solution)/shard_map/all_gather | solution.py:95
  6.5 4.4 %copy-start.1 = (bf16[1024,1024]{1,0:T(8,128)(2,1)S(1)}, bf16[1024,1024]{1,0:T(8,128)(2,1)}, u32[]{:S(2)}) copy-start(bf16[1024,1024]{1,0:T(8,128)(2,1)} %param.12) | copy-start | bytes 6291460
  14.4 1.4 copy-start.2
  15.7 1.5 copy-start.4
  30.5 10.1 %collective-permute-start = (bf16[1024,2,128]{2,0,1:T(8,128)(2,1)}, bf16[1024,2,128]{2,0,1:T(8,128)(2,1)S(1)}, u32[]{:S(2)}, u32[]{:S(2)}) collective-permute-start(bf16[1024,2,128]{2,0,1:T(8,128)(2,1)} %get-tuple-element.802), channel_id=1, source_target_pairs={{0,4},{4,8},{8,12},{12,16},{16,20},{20,24},{24,28},{1,5},{5,9},{9,... | collective-permute-start | bytes 1572872 | tf_op jit(solution)/shard_map/while/body/eval_jaxpr/ppermute | solution.py:10
  34.2 11.9 %collective-permute-start.1 = (bf16[1024,2,128]{0,2,1:T(8,128)(2,1)S(1)}, bf16[1024,2,128]{0,2,1:T(8,128)(2,1)}, u32[]{:S(2)}, u32[]{:S(2)}) collective-permute-start(bf16[1024,2,128]{0,2,1:T(8,128)(2,1)S(1)} %get-tuple-element.803), channel_id=1, source_target_pairs={{0,4},{4,8},{8,12},{12,16},{16,20},{20,24},{24,28},{1,5},{5,9},{9,... | collective-permute-start | bytes 1572872 | tf_op jit(solution)/shard_map/while/body/eval_jaxpr/ppermute | solution.py:10
  60.9 11.8 %collective-permute-start = (bf16[1024,2,128]{2,0,1:T(8,128)(2,1)}, bf16[1024,2,128]{2,0,1:T(8,128)(2,1)S(1)}, u32[]{:S(2)}, u32[]{:S(2)}) collective-permute-start(bf16[1024,2,128]{2,0,1:T(8,128)(2,1)} %get-tuple-element.802), channel_id=1, source_target_pairs={{0,4},{4,8},{8,12},{12,16},{16,20},{20,24},{24,28},{1,5},{5,9},{9,... | collective-permute-start | bytes 1572872 | tf_op jit(solution)/shard_map/while/body/eval_jaxpr/ppermute | solution.py:10
  66.3 11.9 %collective-permute-start.1 = (bf16[1024,2,128]{0,2,1:T(8,128)(2,1)S(1)}, bf16[1024,2,128]{0,2,1:T(8,128)(2,1)}, u32[]{:S(2)}, u32[]{:S(2)}) collective-permute-start(bf16[1024,2,128]{0,2,1:T(8,128)(2,1)S(1)} %get-tuple-element.803), channel_id=1, source_target_pairs={{0,4},{4,8},{8,12},{12,16},{16,20},{20,24},{24,28},{1,5},{5,9},{9,... | collective-permute-start | bytes 1572872 | tf_op jit(solution)/shard_map/while/body/eval_jaxpr/ppermute | solution.py:10
  93.1 3.6 %copy-start.3 = (f32[2,128]{1,0:T(2,128)S(1)}, f32[2,128]{1,0:T(2,128)}, u32[]{:S(2)}) copy-start(f32[2,128]{1,0:T(2,128)} %param.16) | copy-start | bytes 3076
  101.1 26.1 %all-to-all-start = ((bf16[2,128,1024]{1,0,2:T(2,128)(2,1)}), bf16[2,128,1024]{1,0,2:T(2,128)(2,1)S(1)}, u32[]{:S(2)}, u32[]{:S(2)}) async-start(bf16[2,128,1024]{1,0,2:T(2,128)(2,1)} %copy.39), calls=%async_computation | async-start | bytes 1048576 | tf_op jit(solution)/shard_map/all_to_all | solution.py:92
Sparse Core Ops, SparseCore 0:
  99.2 55.7 all-gather.1
where the time goes:
time: 166 us; the launch traced here: 165 us
  waiting for transfers between devices  64.9 us (39%)
  matrix products  33.8 us (20%)
  starting transfers between devices  17.5 us (11%)
  other arithmetic  16.9 us (10%)
  local copies, waits for them, and re-layouts  14.2 us (9%)
  between operations  13.5 us (8%)
  loops' own time  4.27 us (3%)
    all_gather x1, waiting for transfers between devices, on_device(): lax.all_gather(gated, 'narrow', axis=1, tiled=True)  27.4 us
    dot_general x6, matrix products, block_step(): jnp.einsum('hrk,khc->rhc', weights, value_block, preferred_element_type=j...  27.1 us
    ppermute x4, waiting for transfers between devices, from_behind(): lax.ppermute(value, axis, [(source, source + steps) for source in range(i...  20 us
    all_to_all x1, waiting for transfers between devices, on_device(): lax.all_to_all(w_out, 'narrow', split_axis=2, concat_axis=0, tiled=True)  17.5 us
    ppermute x4, starting transfers between devices, from_behind(): lax.ppermute(value, axis, [(source, source + steps) for source in range(i...  12.9 us
    all_to_all x1, starting transfers between devices, on_device(): lax.all_to_all(w_out, 'narrow', split_axis=2, concat_axis=0, tiled=True)  4.59 us
    another operation x3, loops' own time, attend(): lax.scan(block_step, running, jnp.arange(key_count // block_rows, dtype=j...  4.21 us
    convert_element_type x1, other arithmetic, on_device(): events_f = events.astype(jnp.float32)  3.98 us
  transfers between devices with their start and end apart: 6, of which 6 were waited for; matrix products, arithmetic and copies ran while one was open for 4% of the time, Pallas kernels for 0%

commit v1 on v0

--- a/solution.py
+++ b/solution.py
@@ -2,6 +2,27 @@
 import jax.numpy as jnp
 from jax import lax
 from jax.sharding import PartitionSpec as P
+
+
+def in_order(blocks, dim):
+    shape = list(blocks.shape[1:])
+    shape[dim] *= blocks.shape[0]
+    return jnp.moveaxis(blocks, 0, dim).reshape(shape)
+
+
+def doubled(array, axis):
+    size, here = (lax.axis_size(axis), lax.axis_index(axis))
+    tiles, apart = (array[None], 1)
+    while apart < size:
+        theirs = lax.ppermute(tiles, axis, [(i, i ^ apart) for i in range(size)])
+        low = here & apart == 0
+        tiles = jnp.concatenate([jnp.where(low, tiles, theirs), jnp.where(low, theirs, tiles)])
+        apart *= 2
+    return tiles
+
+
+def gather_by_bits(x, axis, dim):
+    return in_order(doubled(x, axis), dim)
 
 
 def from_behind(value, axis, steps):
@@ -92,7 +113,7 @@
     columns = lax.all_to_all(w_out, "narrow", split_axis=2, concat_axis=0, tiled=True)
     summed = jnp.einsum(
         "rhc,hcd->rd",
-        lax.all_gather(gated, "narrow", axis=1, tiled=True),
+        gather_by_bits(gated, "narrow", 1),
         columns,
         preferred_element_type=jnp.float32,
     )

time: 166 us -> 175 us (1.054)
  waiting for transfers between devices: 64.9 us -> 78.4 us
  between operations: 13.5 us -> 0.18 us
  other arithmetic: 16.9 us -> 21 us
  starting transfers between devices: 17.5 us -> 20.6 us
    all_to_all x1, waiting for transfers between devices: 17.5 us -> 46.6 us  [on_device(): lax.all_to_all(w_out, 'narrow', split_axis=2, concat_axis=0, tiled=True)]
    all_gather x1 -> x0, waiting for transfers between devices: 27.4 us -> none  [on_device(): lax.all_gather(gated, 'narrow', axis=1, tiled=True)]
    ppermute x0 -> x2, waiting for transfers between devices: none -> 11.9 us  [doubled(): theirs = lax.ppermute(tiles, axis, [(i, i ^ apart) for i in range(size)])]
    ppermute x0 -> x2, starting transfers between devices: none -> 3.6 us  [doubled(): theirs = lax.ppermute(tiles, axis, [(i, i ^ apart) for i in range(size)])]
    select_n x0 -> x2, other arithmetic: none -> 2.83 us  [doubled(): jnp.where(low, tiles, theirs)]
    broadcast_in_dim x0 -> x1, other arithmetic: none -> 2.36 us  [doubled(): tiles, apart = (array[None], 1)]
    convert_element_type x1 -> x0, other arithmetic: 2.36 us -> none  [on_device(): gated = gated.astype(jnp.bfloat16)]
    unnamed x14 -> x16, local copies, waits for them, and re-layouts: 3.58 us -> 3.6 us
  transfers between devices with their start and end apart: 6 -> 7, of which waited for: 6 -> 6; matrix products, arithmetic and copies ran while one was open for 4% -> 5% of each run, Pallas kernels for 0% -> 0%
where the time goes in v1:
time: 175 us; the launch traced here: 174 us
  waiting for transfers between devices  78.4 us (45%)
  matrix products  33.2 us (19%)
  other arithmetic  21 us (12%)
  starting transfers between devices  20.6 us (12%)
  local copies, waits for them, and re-layouts  15.8 us (9%)
  loops' own time  4.27 us (2%)
    all_to_all x1, waiting for transfers between devices, on_device(): lax.all_to_all(w_out, 'narrow', split_axis=2, concat_axis=0, tiled=True)  46.6 us
    dot_general x6, matrix products, block_step(): jnp.einsum('hrk,khc->rhc', weights, value_block, preferred_element_type=j...  27.1 us
    ppermute x4, waiting for transfers between devices, from_behind(): lax.ppermute(value, axis, [(source, source + steps) for source in range(i...  20 us
    ppermute x4, starting transfers between devices, from_behind(): lax.ppermute(value, axis, [(source, source + steps) for source in range(i...  12.9 us
    ppermute x2, waiting for transfers between devices, doubled(): theirs = lax.ppermute(tiles, axis, [(i, i ^ apart) for i in range(size)])  11.9 us
    another operation x3, loops' own time, attend(): lax.scan(block_step, running, jnp.arange(key_count // block_rows, dtype=j...  4.21 us
    all_to_all x1, starting transfers between devices, on_device(): lax.all_to_all(w_out, 'narrow', split_axis=2, concat_axis=0, tiled=True)  4.13 us
    convert_element_type x1, other arithmetic, on_device(): events_f = events.astype(jnp.float32)  3.98 us
  transfers between devices with their start and end apart: 7, of which 6 were waited for; matrix products, arithmetic and copies ran while one was open for 5% of the time, Pallas kernels for 0%

profile of v1, /device:TPU:3, one launch (start us, length us, event | category | flops | bytes accessed | tf_op | source)
XLA Modules:
  0.0 173.5 jit_solution(4792431687881772204)
XLA Ops:
  0.0 2.1 %convert_reduce_fusion.2 = f32[1024]{0:T(1024)S(1)} fusion(bf16[1024,1024]{1,0:T(8,128)(2,1)} %param.12), kind=kLoop, calls=%fused_computation.47 | loop fusion | flops 2096128 | bytes 2101248 | tf_op jit(solution)/shard_map/reduce_sum | solution.py:43
  2.1 2.3 %multiply_reduce_fusion = f32[1024]{0:T(1024)S(1)} fusion(bf16[1024,1024]{1,0:T(8,128)(2,1)} %param.12, f32[1024]{0:T(1024)S(1)} %broadcast_multiply_fusion.1), kind=kLoop, calls=%fused_computation.46 | loop fusion | flops 4193280 | bytes 2105344 | tf_op jit(solution)/shard_map/reduce_sum | solution.py:44
  4.4 3.4 %multiply_convert_fusion = bf16[1024,2,512]{2,0,1:T(8,128)(2,1)S(1)} fusion(bf16[1024,2,512]{2,1,0:T(2,128)(2,1)S(1)} %copy-done, bf16[1024,1024]{1,0:T(8,128)(2,1)S(1)} %copy-done.1, f32[1024]{0:T(1024)S(1)} %copy-done.6, f32[1024]{0:T(1024)S(1)} %add_rsqrt_fusion.1, f32[1024]{0:T(1024)S(1)} %broadcast_multiply_fusion.1), kind=kOutput, calls=%fused_computation.44 | convolution fusion | flops 2157969408 | bytes 6303744 | tf_op jit(solution)/shard_map/rd,dhc->rhc/dot_general | solution.py:46
  7.9 1.3 copy-done.2
  9.2 1.2 fusion.50
  11.1 12.9 %while.56 = (s32[]{:T(128)}, f32[1024,2,128]{0,2,1:T(8,128)}, s32[2]{0:T(128)S(1)}, bf16[1024,2,128]{0,2,1:T(8,128)(2,1)S(1)}, s32[24]{0:T(128)S(1)}, /*index=5*...) while((s32[]{:T(128)}, f32[1024,2,128]{0,2,1:T(8,128)}, ...), condition=%wide.region_6.7_spmd.clone.clone.clone, body=%wide.region_4.6_spmd.clone.clone.clone.sunk | while | flops 546871296 | bytes 4219704 | solution.py:87
  11.1 0.7 dynamic_slice.51
  13.1 4.2 %fusion.66 = f32[1024,2,128]{0,2,1:T(8,128)} fusion(bf16[1024,2,128]{2,0,1:T(8,128)(2,1)} %get-tuple-element.785, pred[1024,512]{0,1:T(8,128)(4,1)S(1)} %and_and_fusion.4, f32[1024,2,128]{0,2,1:T(8,128)} %get-tuple-element.765, pred[]{:T(512)S(6)} %compare.5, bf16[1024,2,128]{2,0,1:T(8,128)(2,1)} %get-tuple-element.784, s32[]{:T(128)S(6)} %select_n.86, ...), kind=kOutput, calls=%fused_computation.33.clone.1 | convolution fusion | flops 544735232 | bytes 3671552 | tf_op jit(solution)/shard_map/while/body/eval_jaxpr/hrk,khc->rhc/dot_general | solution.py:82
  17.4 0.7 dynamic_slice.51
  19.4 4.6 %fusion.66 = f32[1024,2,128]{0,2,1:T(8,128)} fusion(bf16[1024,2,128]{2,0,1:T(8,128)(2,1)} %get-tuple-element.785, pred[1024,512]{0,1:T(8,128)(4,1)S(1)} %and_and_fusion.4, f32[1024,2,128]{0,2,1:T(8,128)} %get-tuple-element.765, pred[]{:T(512)S(6)} %compare.5, bf16[1024,2,128]{2,0,1:T(8,128)(2,1)} %get-tuple-element.784, s32[]{:T(128)S(6)} %select_n.86, ...), kind=kOutput, calls=%fused_computation.33.clone.1 | convolution fusion | flops 544735232 | bytes 3671552 | tf_op jit(solution)/shard_map/while/body/eval_jaxpr/hrk,khc->rhc/dot_general | solution.py:82
  24.0 62.6 %while.55 = (s32[]{:T(128)}, bf16[1024,2,128]{2,0,1:T(8,128)(2,1)}, bf16[1024,2,128]{0,2,1:T(8,128)(2,1)S(1)}, f32[1024,2,128]{0,2,1:T(8,128)}, s32[]{:T(128)}, ...) while((s32[]{:T(128)}, bf16[1024,2,128]{2,0,1:T(8,128)(2,1)}, ...), condition=%wide.region_11.12_spmd.clone.clone, body=%wide.region_7.11_spmd.clone.clone.sunk | while | flops 546609152 | bytes 10511020 | solution.py:103
  24.0 3.7 %collective-permute-start = (bf16[1024,2,128]{2,0,1:T(8,128)(2,1)}, bf16[1024,2,128]{2,0,1:T(8,128)(2,1)S(1)}, u32[]{:S(2)}, u32[]{:S(2)}) collective-permute-start(bf16[1024,2,128]{2,0,1:T(8,128)(2,1)} %get-tuple-element.806), channel_id=1, source_target_pairs={{0,4},{4,8},{8,12},{12,16},{16,20},{20,24},{24,28},{1,5},{5,9},{9,... | collective-permute-start | bytes 1572872 | tf_op jit(solution)/shard_map/while/body/eval_jaxpr/ppermute | solution.py:31
  27.7 1.9 %collective-permute-start.1 = (bf16[1024,2,128]{0,2,1:T(8,128)(2,1)S(1)}, bf16[1024,2,128]{0,2,1:T(8,128)(2,1)}, u32[]{:S(2)}, u32[]{:S(2)}) collective-permute-start(bf16[1024,2,128]{0,2,1:T(8,128)(2,1)S(1)} %get-tuple-element.807), channel_id=1, source_target_pairs={{0,4},{4,8},{8,12},{12,16},{16,20},{20,24},{24,28},{1,5},{5,9},{9,... | collective-permute-start | bytes 1572872 | tf_op jit(solution)/shard_map/while/body/eval_jaxpr/ppermute | solution.py:31
  29.6 4.5 %collective-permute-done = bf16[1024,2,128]{2,0,1:T(8,128)(2,1)S(1)} collective-permute-done((bf16[1024,2,128]{2,0,1:T(8,128)(2,1)}, bf16[1024,2,128]{2,0,1:T(8,128)(2,1)S(1)}, u32[]{:S(2)}, u32[]{:S(2)}) %collective-permute-start) | collective-permute-done | bytes 524320 | tf_op jit(solution)/shard_map/while/body/eval_jaxpr/ppermute | solution.py:31
  34.1 5.5 %collective-permute-done.1 = bf16[1024,2,128]{0,2,1:T(8,128)(2,1)} collective-permute-done((bf16[1024,2,128]{0,2,1:T(8,128)(2,1)S(1)}, bf16[1024,2,128]{0,2,1:T(8,128)(2,1)}, u32[]{:S(2)}, u32[]{:S(2)}) %collective-permute-start.1) | collective-permute-done | bytes 524320 | tf_op jit(solution)/shard_map/while/body/eval_jaxpr/ppermute | solution.py:31
  39.6 13.0 %while.57 = (s32[]{:T(128)}, f32[1024,2,128]{0,2,1:T(8,128)}, s32[2]{0:T(128)S(1)}, bf16[1024,2,128]{0,2,1:T(8,128)(2,1)}, s32[24]{0:T(128)S(1)}, /*index=5*/s32...) while((s32[]{:T(128)}, f32[1024,2,128]{0,2,1:T(8,128)}, ...), condition=%wide.region_10.10_spmd, body=%wide.region_8.9_spmd.sunk | while | flops 546608128 | bytes 4215091 | solution.py:87
  39.6 0.6 dynamic_slice.54
  41.5 4.6 %fusion.70 = f32[1024,2,128]{0,2,1:T(8,128)} fusion(f32[1024,2,128]{0,2,1:T(8,128)} %get-tuple-element.724, bf16[1024,2,128]{2,0,1:T(8,128)(2,1)} %get-tuple-element.746, pred[1024,512]{0,1:T(8,128)(4,1)S(1)} %and_and_fusion.5, bf16[1024,2,128]{2,0,1:T(8,128)(2,1)S(1)} %get-tuple-element.745, s32[]{:T(128)S(6)} %select_n.88, ...), kind=kOutput, calls=%fused_computation.12.clone.1 | convolution fusion | flops 544473088 | bytes 3671040 | tf_op jit(solution)/shard_map/while/body/eval_jaxpr/while/body/eval_jaxpr/hrk,khc->rhc/dot_general | solution.py:82
  46.1 0.6 dynamic_slice.54
  48.0 4.6 %fusion.70 = f32[1024,2,128]{0,2,1:T(8,128)} fusion(f32[1024,2,128]{0,2,1:T(8,128)} %get-tuple-element.724, bf16[1024,2,128]{2,0,1:T(8,128)(2,1)} %get-tuple-element.746, pred[1024,512]{0,1:T(8,128)(4,1)S(1)} %and_and_fusion.5, bf16[1024,2,128]{2,0,1:T(8,128)(2,1)S(1)} %get-tuple-element.745, s32[]{:T(128)S(6)} %select_n.88, ...), kind=kOutput, calls=%fused_computation.12.clone.1 | convolution fusion | flops 544473088 | bytes 3671040 | tf_op jit(solution)/shard_map/while/body/eval_jaxpr/while/body/eval_jaxpr/hrk,khc->rhc/dot_general | solution.py:82
  52.6 0.8 copy.68
  53.4 1.0 copy.69
  54.4 5.4 %collective-permute-start = (bf16[1024,2,128]{2,0,1:T(8,128)(2,1)}, bf16[1024,2,128]{2,0,1:T(8,128)(2,1)S(1)}, u32[]{:S(2)}, u32[]{:S(2)}) collective-permute-start(bf16[1024,2,128]{2,0,1:T(8,128)(2,1)} %get-tuple-element.806), channel_id=1, source_target_pairs={{0,4},{4,8},{8,12},{12,16},{16,20},{20,24},{24,28},{1,5},{5,9},{9,... | collective-permute-start | bytes 1572872 | tf_op jit(solution)/shard_map/while/body/eval_jaxpr/ppermute | solution.py:31
  59.8 1.9 %collective-permute-start.1 = (bf16[1024,2,128]{0,2,1:T(8,128)(2,1)S(1)}, bf16[1024,2,128]{0,2,1:T(8,128)(2,1)}, u32[]{:S(2)}, u32[]{:S(2)}) collective-permute-start(bf16[1024,2,128]{0,2,1:T(8,128)(2,1)S(1)} %get-tuple-element.807), channel_id=1, source_target_pairs={{0,4},{4,8},{8,12},{12,16},{16,20},{20,24},{24,28},{1,5},{5,9},{9,... | collective-permute-start | bytes 1572872 | tf_op jit(solution)/shard_map/while/body/eval_jaxpr/ppermute | solution.py:31
  61.8 4.5 %collective-permute-done = bf16[1024,2,128]{2,0,1:T(8,128)(2,1)S(1)} collective-permute-done((bf16[1024,2,128]{2,0,1:T(8,128)(2,1)}, bf16[1024,2,128]{2,0,1:T(8,128)(2,1)S(1)}, u32[]{:S(2)}, u32[]{:S(2)}) %collective-permute-start) | collective-permute-done | bytes 524320 | tf_op jit(solution)/shard_map/while/body/eval_jaxpr/ppermute | solution.py:31
  66.2 5.5 %collective-permute-done.1 = bf16[1024,2,128]{0,2,1:T(8,128)(2,1)} collective-permute-done((bf16[1024,2,128]{0,2,1:T(8,128)(2,1)S(1)}, bf16[1024,2,128]{0,2,1:T(8,128)(2,1)}, u32[]{:S(2)}, u32[]{:S(2)}) %collective-permute-start.1) | collective-permute-done | bytes 524320 | tf_op jit(solution)/shard_map/while/body/eval_jaxpr/ppermute | solution.py:31
  71.8 13.0 %while.57 = (s32[]{:T(128)}, f32[1024,2,128]{0,2,1:T(8,128)}, s32[2]{0:T(128)S(1)}, bf16[1024,2,128]{0,2,1:T(8,128)(2,1)}, s32[24]{0:T(128)S(1)}, /*index=5*/s32...) while((s32[]{:T(128)}, f32[1024,2,128]{0,2,1:T(8,128)}, ...), condition=%wide.region_10.10_spmd, body=%wide.region_8.9_spmd.sunk | while | flops 546608128 | bytes 4215091 | solution.py:87
  71.8 0.6 dynamic_slice.54
  73.7 4.6 %fusion.70 = f32[1024,2,128]{0,2,1:T(8,128)} fusion(f32[1024,2,128]{0,2,1:T(8,128)} %get-tuple-element.724, bf16[1024,2,128]{2,0,1:T(8,128)(2,1)} %get-tuple-element.746, pred[1024,512]{0,1:T(8,128)(4,1)S(1)} %and_and_fusion.5, bf16[1024,2,128]{2,0,1:T(8,128)(2,1)S(1)} %get-tuple-element.745, s32[]{:T(128)S(6)} %select_n.88, ...), kind=kOutput, calls=%fused_computation.12.clone.1 | convolution fusion | flops 544473088 | bytes 3671040 | tf_op jit(solution)/shard_map/while/body/eval_jaxpr/while/body/eval_jaxpr/hrk,khc->rhc/dot_general | solution.py:82
  80.2 4.6 %fusion.70 = f32[1024,2,128]{0,2,1:T(8,128)} fusion(f32[1024,2,128]{0,2,1:T(8,128)} %get-tuple-element.724, bf16[1024,2,128]{2,0,1:T(8,128)(2,1)} %get-tuple-element.746, pred[1024,512]{0,1:T(8,128)(4,1)S(1)} %and_and_fusion.5, bf16[1024,2,128]{2,0,1:T(8,128)(2,1)S(1)} %get-tuple-element.745, s32[]{:T(128)S(6)} %select_n.88, ...), kind=kOutput, calls=%fused_computation.12.clone.1 | convolution fusion | flops 544473088 | bytes 3671040 | tf_op jit(solution)/shard_map/while/body/eval_jaxpr/while/body/eval_jaxpr/hrk,khc->rhc/dot_general | solution.py:82
  84.8 0.8 copy.68
  85.6 1.0 copy.69
  86.6 1.6 copy.38
  88.2 1.3 reduce_sum.66
  89.5 0.6 multiply_reduce_fusion.1
  90.2 2.4 %fusion.49 = bf16[1,1024,2,128]{3,1,2,0:T(8,128)(2,1)} fusion(f32[1024,2,128]{2,0,1:T(8,128)S(1)} %copy.38, bf16[1024,2,512]{2,0,1:T(8,128)(2,1)} %copy-done.2, f32[2,128]{1,0:T(2,128)S(1)} %copy-done.4, f32[1024,2]{0,1:T(2,128)S(1)} %add_rsqrt_fusion, f32[1024,2]{0,1:T(2,128)S(1)} %broadcast_multiply_fusion), kind=kLoop, calls=%fused_computation.63 | loop fusion | flops 1572864 | bytes 2114560 | tf_op jit(solution)/shard_map/broadcast_in_dim | solution.py:15
  92.5 1.3 collective-permute-start.2
  93.8 11.9 %collective-permute-done.2 = bf16[1,1024,2,128]{3,1,2,0:T(8,128)(2,1)} collective-permute-done((bf16[1,1024,2,128]{3,1,2,0:T(8,128)(2,1)}, bf16[1,1024,2,128]{3,1,2,0:T(8,128)(2,1)}, u32[]{:S(2)}, u32[]{:S(2)}) %collective-permute-start.2) | collective-permute-done | bytes 524320 | tf_op jit(solution)/shard_map/ppermute | solution.py:17
  105.7 1.3 broadcast_select_fusion.3
  107.0 1.1 pad_maximum_fusion.1
  108.1 2.3 %collective-permute-start.3 = (bf16[2,1024,2,128]{3,1,2,0:T(8,128)(2,1)}, bf16[2,1024,2,128]{3,1,2,0:T(8,128)(2,1)}, u32[]{:S(2)}, u32[]{:S(2)}) collective-permute-start(bf16[2,1024,2,128]{3,1,2,0:T(8,128)(2,1)} %pad_maximum_fusion.1), channel_id=1, source_target_pairs={{0,2},{1,3},{2,0},{3,1},{4,6},{5,7},{6,4},{7,5},{8,10},{9,11},{10,... | collective-permute-start | bytes 3145736 | tf_op jit(solution)/shard_map/ppermute | solution.py:17
  110.4 2.0 %copy.39 = bf16[2,128,1024]{1,0,2:T(2,128)(2,1)} copy(bf16[2,128,1024]{2,1,0:T(8,128)(2,1)} %param.17) | data formatting | bytes 1048576 | tf_op args[5]
  112.4 4.1 %all-to-all-start = ((bf16[2,128,1024]{1,0,2:T(2,128)(2,1)}), bf16[2,128,1024]{1,0,2:T(2,128)(2,1)}, u32[]{:S(2)}, u32[]{:S(2)}) async-start(bf16[2,128,1024]{1,0,2:T(2,128)(2,1)} %copy.39), calls=%async_computation | async-start | bytes 1048576 | tf_op jit(solution)/shard_map/all_to_all | solution.py:113
  116.5 4.0 %convert_element_type.33 = f32[1024,1024]{1,0:T(8,128)} convert(bf16[1024,1024]{1,0:T(8,128)(2,1)} %param.12) | non-fusion elementwise | flops 1048576 | bytes 6291456 | tf_op jit(solution)/shard_map/convert_element_type | solution.py:42
  120.5 46.6 %all-to-all-done = bf16[2,128,1024]{1,0,2:T(2,128)(2,1)} async-done(((bf16[2,128,1024]{1,0,2:T(2,128)(2,1)}), bf16[2,128,1024]{1,0,2:T(2,128)(2,1)}, u32[]{:S(2)}, u32[]{:S(2)}) %all-to-all-start) | async-done | bytes 524320 | tf_op jit(solution)/shard_map/all_to_all | solution.py:113
  167.1 2.0 %copy.40 = bf16[2,128,4,256]{3,1,0,2:T(8,128)(2,1)} copy(bf16[2,128,4,256]{1,0,3,2:T(2,128)(2,1)} %bitcast.8) | data formatting | bytes 1048576 | tf_op jit(solution)/shard_map/all_to_all | solution.py:113
  169.0 1.6 broadcast_select_fusion.1
  170.8 2.7 %fusion.48 = bf16[1024,256]{1,0:T(8,128)(2,1)} fusion(bf16[1024,8,128]{2,0,1:T(8,128)(2,1)S(1)} %bitcast.93, bf16[8,128,256]{2,1,0:T(8,128)(2,1)S(1)} %bitcast.94, f32[1024,1024]{1,0:T(8,128)} %convert_element_type.33, s32[]{:T(128)S(6)} %select_n.42), kind=kOutput, calls=%fused_computation.57 | convolution fusion | flops 537395200 | bytes 4194308 | tf_op jit(solution)/shard_map/rhc,hcd->rd/dot_general | solution.py:114
  (58 shorter events, 5.4 us)
Async XLA Ops:
  0.0 4.4 %copy-start = (bf16[1024,2,512]{2,1,0:T(2,128)(2,1)S(1)}, bf16[1024,2,512]{2,1,0:T(2,128)(2,1)}, u32[]{:S(2)}) copy-start(bf16[1024,2,512]{2,1,0:T(2,128)(2,1)} %param.15) | copy-start | bytes 6291460
  0.0 4.4 %copy-start.6 = (f32[1024]{0:T(1024)S(1)}, f32[1024]{0:T(1024)}, u32[]{:S(2)}) copy-start(f32[1024]{0:T(1024)} %param.14) | copy-start | bytes 12292
  0.0 4.4 %copy-start.1 = (bf16[1024,1024]{1,0:T(8,128)(2,1)S(1)}, bf16[1024,1024]{1,0:T(8,128)(2,1)}, u32[]{:S(2)}) copy-start(bf16[1024,1024]{1,0:T(8,128)(2,1)} %param.12) | copy-start | bytes 6291460
  7.9 1.4 copy-start.2
  9.2 1.5 copy-start.5
  24.0 10.1 %collective-permute-start = (bf16[1024,2,128]{2,0,1:T(8,128)(2,1)}, bf16[1024,2,128]{2,0,1:T(8,128)(2,1)S(1)}, u32[]{:S(2)}, u32[]{:S(2)}) collective-permute-start(bf16[1024,2,128]{2,0,1:T(8,128)(2,1)} %get-tuple-element.806), channel_id=1, source_target_pairs={{0,4},{4,8},{8,12},{12,16},{16,20},{20,24},{24,28},{1,5},{5,9},{9,... | collective-permute-start | bytes 1572872 | tf_op jit(solution)/shard_map/while/body/eval_jaxpr/ppermute | solution.py:31
  27.7 11.9 %collective-permute-start.1 = (bf16[1024,2,128]{0,2,1:T(8,128)(2,1)S(1)}, bf16[1024,2,128]{0,2,1:T(8,128)(2,1)}, u32[]{:S(2)}, u32[]{:S(2)}) collective-permute-start(bf16[1024,2,128]{0,2,1:T(8,128)(2,1)S(1)} %get-tuple-element.807), channel_id=1, source_target_pairs={{0,4},{4,8},{8,12},{12,16},{16,20},{20,24},{24,28},{1,5},{5,9},{9,... | collective-permute-start | bytes 1572872 | tf_op jit(solution)/shard_map/while/body/eval_jaxpr/ppermute | solution.py:31
  54.4 11.8 %collective-permute-start = (bf16[1024,2,128]{2,0,1:T(8,128)(2,1)}, bf16[1024,2,128]{2,0,1:T(8,128)(2,1)S(1)}, u32[]{:S(2)}, u32[]{:S(2)}) collective-permute-start(bf16[1024,2,128]{2,0,1:T(8,128)(2,1)} %get-tuple-element.806), channel_id=1, source_target_pairs={{0,4},{4,8},{8,12},{12,16},{16,20},{20,24},{24,28},{1,5},{5,9},{9,... | collective-permute-start | bytes 1572872 | tf_op jit(solution)/shard_map/while/body/eval_jaxpr/ppermute | solution.py:31
  59.8 11.9 %collective-permute-start.1 = (bf16[1024,2,128]{0,2,1:T(8,128)(2,1)S(1)}, bf16[1024,2,128]{0,2,1:T(8,128)(2,1)}, u32[]{:S(2)}, u32[]{:S(2)}) collective-permute-start(bf16[1024,2,128]{0,2,1:T(8,128)(2,1)S(1)} %get-tuple-element.807), channel_id=1, source_target_pairs={{0,4},{4,8},{8,12},{12,16},{16,20},{20,24},{24,28},{1,5},{5,9},{9,... | collective-permute-start | bytes 1572872 | tf_op jit(solution)/shard_map/while/body/eval_jaxpr/ppermute | solution.py:31
  86.6 3.6 %copy-start.4 = (f32[2,128]{1,0:T(2,128)S(1)}, f32[2,128]{1,0:T(2,128)}, u32[]{:S(2)}) copy-start(f32[2,128]{1,0:T(2,128)} %param.16) | copy-start | bytes 3076
  92.5 13.2 %collective-permute-start.2 = (bf16[1,1024,2,128]{3,1,2,0:T(8,128)(2,1)}, bf16[1,1024,2,128]{3,1,2,0:T(8,128)(2,1)}, u32[]{:S(2)}, u32[]{:S(2)}) collective-permute-start(bf16[1,1024,2,128]{3,1,2,0:T(8,128)(2,1)} %fusion.49), channel_id=1, source_target_pairs={{0,1},{1,0},{2,3},{3,2},{4,5},{5,4},{6,7},{7,6},{8,9},{9,8},{10,11... | collective-permute-start | bytes 1572872 | tf_op jit(solution)/shard_map/ppermute | solution.py:17
  108.1 61.0 %collective-permute-start.3 = (bf16[2,1024,2,128]{3,1,2,0:T(8,128)(2,1)}, bf16[2,1024,2,128]{3,1,2,0:T(8,128)(2,1)}, u32[]{:S(2)}, u32[]{:S(2)}) collective-permute-start(bf16[2,1024,2,128]{3,1,2,0:T(8,128)(2,1)} %pad_maximum_fusion.1), channel_id=1, source_target_pairs={{0,2},{1,3},{2,0},{3,1},{4,6},{5,7},{6,4},{7,5},{8,10},{9,11},{10,... | collective-permute-start | bytes 3145736 | tf_op jit(solution)/shard_map/ppermute | solution.py:17
  112.4 54.7 %all-to-all-start = ((bf16[2,128,1024]{1,0,2:T(2,128)(2,1)}), bf16[2,128,1024]{1,0,2:T(2,128)(2,1)}, u32[]{:S(2)}, u32[]{:S(2)}) async-start(bf16[2,128,1024]{1,0,2:T(2,128)(2,1)} %copy.39), calls=%async_computation | async-start | bytes 1048576 | tf_op jit(solution)/shard_map/all_to_all | solution.py:113
  169.0 1.8 %copy-start.3 = (bf16[2,128,4,256]{3,1,0,2:T(8,128)(2,1)S(1)}, bf16[2,128,4,256]{3,1,0,2:T(8,128)(2,1)}, u32[]{:S(2)}) copy-start(bf16[2,128,4,256]{3,1,0,2:T(8,128)(2,1)} %copy.40) | copy-start | bytes 1572868
